TPU v7x, 32 devices: a whole 2x2x4 slice. The times are simulated.
32 devices in a mesh: pipe: 4 (over y, x), ctx: 8 (over z, core).
Axes of the slice: x: 2, y: 2, z: 4, core: 2. Of those that a mesh axis runs over, the one named last changes fastest.
Arguments:
- queries: bfloat16 [4, 1, 1024, 3072], P('pipe', None, 'ctx'), may hold values from -24 to 24
- projected_key_value: bfloat16 [4, 1, 1024, 1024], P('pipe', None, 'ctx'), may hold values from -24 to 24
- layout: int32 [1, 1, 16], replicated, may hold values from 0 to 15, each once within a row
Outputs:
- arrived: bfloat16 [4, 1, 1024, 3072], P('pipe', None, 'ctx')
Inputs may be any that keep to these rules, and one draw needn't show every extreme that they name: Every row of layout names each of the 16 token blocks once.
All inputs are finite; a program needn't handle non-finite values.
Results may differ from a plain program's by a relative error of at most 0.0055.
Values may be sent and summed in bfloat16 or wider, within the bound.
A program may use at most 64 MiB of HBM per device.

v0:
```python
import math

import jax
import jax.numpy as jnp
from jax import lax
from jax.sharding import PartitionSpec as P

KEY_VALUE_HEADS = 4
HEAD_SIZE = 128
QUERY_PER_KV = 6


def shifted(array, axis, by):
    peers = lax.axis_size(axis)
    return lax.ppermute(array, axis, [(i, (i + by) % peers) for i in range(peers)])


def owner_positions(table_row, owner, tokens_per_member, block_rows):
    rows_iota = jnp.arange(tokens_per_member, dtype=jnp.int32)
    slots = 2 * owner + rows_iota // block_rows
    columns = jnp.arange(table_row.shape[0], dtype=jnp.int32)
    picked = jnp.sum(jnp.where(slots[:, None] == columns[None, :], table_row[None, :], 0), axis=1)
    return picked * block_rows + rows_iota % block_rows


def tile_update(state, query_rows, query_pos, key_rows, value_rows, key_pos):
    run_max, run_total, accum = state
    score_scale = 1.0 / math.sqrt(HEAD_SIZE)
    scores = (
        jnp.einsum("ihgd,jhd->hgij", query_rows, key_rows, preferred_element_type=jnp.float32)
        * score_scale
    )
    allowed = key_pos[None, :] <= query_pos[:, None]
    scores = jnp.where(allowed[None, None], scores, -1e30)
    new_max = jnp.maximum(run_max, jnp.max(scores, axis=3))
    expo = jnp.exp(scores - new_max[..., None])
    factor = jnp.exp(run_max - new_max)
    new_total = run_total * factor + jnp.sum(expo, axis=3)
    weights = expo.astype(jnp.bfloat16)
    product = jnp.einsum("hgij,jhd->ihgd", weights, value_rows, preferred_element_type=jnp.float32)
    accum = accum * jnp.transpose(factor, (2, 0, 1))[..., None] + product
    return (new_max, new_total, accum)


def attend_piece(carry, query_tile_rows, query_pos, token_portion, piece_pos):
    key_value_width = token_portion.shape[1] // 2
    key_tile_rows = token_portion[:, :key_value_width].reshape(
        token_portion.shape[0], KEY_VALUE_HEADS, HEAD_SIZE
    )
    value_tile_rows = token_portion[:, key_value_width:].reshape(
        token_portion.shape[0], KEY_VALUE_HEADS, HEAD_SIZE
    )
    return tile_update(carry, query_tile_rows, query_pos, key_tile_rows, value_tile_rows, piece_pos)


def on_device(queries, projected_key_value, layout):
    tokens_per_member = queries.shape[2]
    width = queries.shape[3]
    block_rows = tokens_per_member // 2
    seq_devs = layout.shape[2] // 2
    cycle_index = lax.axis_index("ctx")
    local = cycle_index % seq_devs
    sequence = cycle_index // seq_devs
    tables = lax.dynamic_index_in_dim(layout, sequence, 1, keepdims=False)
    query_tile_rows = queries[0, 0].reshape(
        tokens_per_member, KEY_VALUE_HEADS, QUERY_PER_KV, HEAD_SIZE
    )
    own_piece = projected_key_value[0, 0]
    table_row = tables[0]
    query_pos = owner_positions(table_row, local, tokens_per_member, block_rows)
    start = (
        jnp.full((KEY_VALUE_HEADS, QUERY_PER_KV, tokens_per_member), -1e30, jnp.float32),
        jnp.zeros((KEY_VALUE_HEADS, QUERY_PER_KV, tokens_per_member), jnp.float32),
        jnp.zeros((tokens_per_member, KEY_VALUE_HEADS, QUERY_PER_KV, HEAD_SIZE), jnp.float32),
    )
    carry = attend_piece(start, query_tile_rows, query_pos, own_piece, query_pos)

    def cycle_hop(hop_index, state):
        travel, inner = state
        travel = shifted(travel, "ctx", 1)
        owner = (local - hop_index) % seq_devs
        piece_pos = owner_positions(table_row, owner, tokens_per_member, block_rows)
        inner = attend_piece(inner, query_tile_rows, query_pos, travel, piece_pos)
        return (travel, inner)

    carry = lax.fori_loop(1, seq_devs, cycle_hop, (own_piece, carry))[1]
    run_max, run_total, accum = carry
    attended = (
        (accum / jnp.transpose(run_total, (2, 0, 1))[..., None])
        .astype(jnp.bfloat16)
        .reshape(tokens_per_member, width)
    )
    results = [shifted(attended, "pipe", 1)]
    return jnp.stack(results)[None]


def solution(mesh):
    placed = (P("pipe", None, "ctx", None), P("pipe", None, "ctx", None), P())
    return jax.shard_map(
        on_device,
        mesh=mesh,
        in_specs=placed,
        out_specs=P("pipe", None, "ctx", None),
        check_vma=False,
    )
```

profile of v0, /device:TPU:0, one launch (start us, length us, event | category | flops | bytes accessed | tf_op | source)
XLA Modules:
  0.0 88.7 jit_solution(3103879223213215892)
XLA Ops:
  0.0 0.8 select_reduce_fusion.1
  0.8 0.1 broadcast_compare_fusion.1
  0.9 1.1 %copy.22 = bf16[1,1,128,1024]{2,3,1,0:T(8,128)(2,1)S(1)} copy(bf16[1,1,128,1024]{3,2,1,0:T(8,128)(2,1)} %param.6) | data formatting | bytes 524288 | tf_op args[1]
  2.1 0.4 copy.23
  2.5 0.4 copy.28
  2.9 0.4 fusion.18
  3.3 0.3 fusion.8
  3.6 0.0 copy-start.1
  3.6 0.8 bitcast_add_fusion.1
  4.5 67.8 %while.22 = (s32[]{:T(128)}, bf16[128,1024]{0,1:T(8,128)(2,1)S(1)}, f32[4,6,128]{2,1,0:T(8,128)S(1)}, f32[4,6,128]{2,1,0:T(8,128)S(1)}, f32[128,4,6,128]{3,0,2,1...) while((s32[]{:T(128)}, bf16[128,1024]{0,1:T(8,128)(2,1)S(1)}, ...), condition=%wide.region_7.8_spmd, body=%wide.region_3.7_spmd.sunk | while | flops 204899344 | bytes 11243382 | solution.py:86
  4.5 0.5 collective-permute-start
  5.1 0.1 select_reduce_fusion.3
  5.2 0.1 broadcast_compare_fusion.3
  5.3 7.9 %collective-permute-done = bf16[128,1024]{0,1:T(8,128)(2,1)S(1)} collective-permute-done((bf16[128,1024]{0,1:T(8,128)(2,1)S(1)}, bf16[128,1024]{0,1:T(8,128)(2,1)S(1)}, u32[]{:S(2)}, u32[]{:S(2)}) %collective-permute-start) | collective-permute-done | bytes 262176 | tf_op jit(solution)/shard_map/while/body/eval_jaxpr/ppermute | solution.py:15
  13.2 0.4 fusion.42
  13.6 0.3 fusion.44
  14.0 1.0 %bitcast_add_fusion.3 = f32[128,4,6,128]{3,0,2,1:T(8,128)S(1)} fusion(f32[128,4,6,128]{3,0,2,1:T(8,128)S(1)} %get-tuple-element.397, bf16[128,4,128,1]{0,2,3,1:T(8,128)(2,1)S(1)} %bitcast.62, f32[4,6,128,128]{2,3,1,0:T(8,128)S(1)} %get-tuple-element.376, f32[128,4,6]{0,2,1:T(8,128)S(1)} %get-tuple-element.378, f32[4,6,128]{2,1,0:T(8,128)S(1)} %get-tuple-element.409), kind=kOutput, calls=%fused_computation.clone.1 | convolution fusion | flops 102236160 | bytes 4874240 | tf_op jit(solution)/shard_map/while/body/eval_jaxpr/hgij,jhd->ihgd/dot_general | solution.py:40
  15.0 0.1 collective-permute-start
  15.1 0.1 select_reduce_fusion.3
  15.2 0.1 broadcast_compare_fusion.3
  15.3 7.4 %collective-permute-done = bf16[128,1024]{0,1:T(8,128)(2,1)S(1)} collective-permute-done((bf16[128,1024]{0,1:T(8,128)(2,1)S(1)}, bf16[128,1024]{0,1:T(8,128)(2,1)S(1)}, u32[]{:S(2)}, u32[]{:S(2)}) %collective-permute-start) | collective-permute-done | bytes 262176 | tf_op jit(solution)/shard_map/while/body/eval_jaxpr/ppermute | solution.py:15
  22.7 0.4 fusion.42
  23.2 0.3 fusion.44
  23.5 1.0 %bitcast_add_fusion.3 = f32[128,4,6,128]{3,0,2,1:T(8,128)S(1)} fusion(f32[128,4,6,128]{3,0,2,1:T(8,128)S(1)} %get-tuple-element.397, bf16[128,4,128,1]{0,2,3,1:T(8,128)(2,1)S(1)} %bitcast.62, f32[4,6,128,128]{2,3,1,0:T(8,128)S(1)} %get-tuple-element.376, f32[128,4,6]{0,2,1:T(8,128)S(1)} %get-tuple-element.378, f32[4,6,128]{2,1,0:T(8,128)S(1)} %get-tuple-element.409), kind=kOutput, calls=%fused_computation.clone.1 | convolution fusion | flops 102236160 | bytes 4874240 | tf_op jit(solution)/shard_map/while/body/eval_jaxpr/hgij,jhd->ihgd/dot_general | solution.py:40
  24.6 0.1 collective-permute-start
  24.7 0.1 select_reduce_fusion.3
  24.8 0.1 broadcast_compare_fusion.3
  24.9 7.4 %collective-permute-done = bf16[128,1024]{0,1:T(8,128)(2,1)S(1)} collective-permute-done((bf16[128,1024]{0,1:T(8,128)(2,1)S(1)}, bf16[128,1024]{0,1:T(8,128)(2,1)S(1)}, u32[]{:S(2)}, u32[]{:S(2)}) %collective-permute-start) | collective-permute-done | bytes 262176 | tf_op jit(solution)/shard_map/while/body/eval_jaxpr/ppermute | solution.py:15
  32.2 0.4 fusion.42
  32.7 0.3 fusion.44
  33.0 1.0 %bitcast_add_fusion.3 = f32[128,4,6,128]{3,0,2,1:T(8,128)S(1)} fusion(f32[128,4,6,128]{3,0,2,1:T(8,128)S(1)} %get-tuple-element.397, bf16[128,4,128,1]{0,2,3,1:T(8,128)(2,1)S(1)} %bitcast.62, f32[4,6,128,128]{2,3,1,0:T(8,128)S(1)} %get-tuple-element.376, f32[128,4,6]{0,2,1:T(8,128)S(1)} %get-tuple-element.378, f32[4,6,128]{2,1,0:T(8,128)S(1)} %get-tuple-element.409), kind=kOutput, calls=%fused_computation.clone.1 | convolution fusion | flops 102236160 | bytes 4874240 | tf_op jit(solution)/shard_map/while/body/eval_jaxpr/hgij,jhd->ihgd/dot_general | solution.py:40
  34.1 0.1 collective-permute-start
  34.2 0.1 select_reduce_fusion.3
  34.3 0.1 broadcast_compare_fusion.3
  34.4 7.4 %collective-permute-done = bf16[128,1024]{0,1:T(8,128)(2,1)S(1)} collective-permute-done((bf16[128,1024]{0,1:T(8,128)(2,1)S(1)}, bf16[128,1024]{0,1:T(8,128)(2,1)S(1)}, u32[]{:S(2)}, u32[]{:S(2)}) %collective-permute-start) | collective-permute-done | bytes 262176 | tf_op jit(solution)/shard_map/while/body/eval_jaxpr/ppermute | solution.py:15
  41.8 0.4 fusion.42
  42.3 0.3 fusion.44
  42.6 1.0 %bitcast_add_fusion.3 = f32[128,4,6,128]{3,0,2,1:T(8,128)S(1)} fusion(f32[128,4,6,128]{3,0,2,1:T(8,128)S(1)} %get-tuple-element.397, bf16[128,4,128,1]{0,2,3,1:T(8,128)(2,1)S(1)} %bitcast.62, f32[4,6,128,128]{2,3,1,0:T(8,128)S(1)} %get-tuple-element.376, f32[128,4,6]{0,2,1:T(8,128)S(1)} %get-tuple-element.378, f32[4,6,128]{2,1,0:T(8,128)S(1)} %get-tuple-element.409), kind=kOutput, calls=%fused_computation.clone.1 | convolution fusion | flops 102236160 | bytes 4874240 | tf_op jit(solution)/shard_map/while/body/eval_jaxpr/hgij,jhd->ihgd/dot_general | solution.py:40
  43.7 0.1 collective-permute-start
  43.8 0.1 select_reduce_fusion.3
  43.8 0.1 broadcast_compare_fusion.3
  43.9 7.4 %collective-permute-done = bf16[128,1024]{0,1:T(8,128)(2,1)S(1)} collective-permute-done((bf16[128,1024]{0,1:T(8,128)(2,1)S(1)}, bf16[128,1024]{0,1:T(8,128)(2,1)S(1)}, u32[]{:S(2)}, u32[]{:S(2)}) %collective-permute-start) | collective-permute-done | bytes 262176 | tf_op jit(solution)/shard_map/while/body/eval_jaxpr/ppermute | solution.py:15
  51.3 0.4 fusion.42
  51.8 0.3 fusion.44
  52.1 1.0 %bitcast_add_fusion.3 = f32[128,4,6,128]{3,0,2,1:T(8,128)S(1)} fusion(f32[128,4,6,128]{3,0,2,1:T(8,128)S(1)} %get-tuple-element.397, bf16[128,4,128,1]{0,2,3,1:T(8,128)(2,1)S(1)} %bitcast.62, f32[4,6,128,128]{2,3,1,0:T(8,128)S(1)} %get-tuple-element.376, f32[128,4,6]{0,2,1:T(8,128)S(1)} %get-tuple-element.378, f32[4,6,128]{2,1,0:T(8,128)S(1)} %get-tuple-element.409), kind=kOutput, calls=%fused_computation.clone.1 | convolution fusion | flops 102236160 | bytes 4874240 | tf_op jit(solution)/shard_map/while/body/eval_jaxpr/hgij,jhd->ihgd/dot_general | solution.py:40
  53.2 0.1 collective-permute-start
  53.3 0.1 select_reduce_fusion.3
  53.4 0.1 broadcast_compare_fusion.3
  53.5 7.4 %collective-permute-done = bf16[128,1024]{0,1:T(8,128)(2,1)S(1)} collective-permute-done((bf16[128,1024]{0,1:T(8,128)(2,1)S(1)}, bf16[128,1024]{0,1:T(8,128)(2,1)S(1)}, u32[]{:S(2)}, u32[]{:S(2)}) %collective-permute-start) | collective-permute-done | bytes 262176 | tf_op jit(solution)/shard_map/while/body/eval_jaxpr/ppermute | solution.py:15
  60.9 0.4 fusion.42
  61.3 0.3 fusion.44
  61.7 1.0 %bitcast_add_fusion.3 = f32[128,4,6,128]{3,0,2,1:T(8,128)S(1)} fusion(f32[128,4,6,128]{3,0,2,1:T(8,128)S(1)} %get-tuple-element.397, bf16[128,4,128,1]{0,2,3,1:T(8,128)(2,1)S(1)} %bitcast.62, f32[4,6,128,128]{2,3,1,0:T(8,128)S(1)} %get-tuple-element.376, f32[128,4,6]{0,2,1:T(8,128)S(1)} %get-tuple-element.378, f32[4,6,128]{2,1,0:T(8,128)S(1)} %get-tuple-element.409), kind=kOutput, calls=%fused_computation.clone.1 | convolution fusion | flops 102236160 | bytes 4874240 | tf_op jit(solution)/shard_map/while/body/eval_jaxpr/hgij,jhd->ihgd/dot_general | solution.py:40
  62.7 0.1 collective-permute-start
  62.8 0.1 select_reduce_fusion.3
  62.9 0.1 broadcast_compare_fusion.3
  63.0 7.4 %collective-permute-done = bf16[128,1024]{0,1:T(8,128)(2,1)S(1)} collective-permute-done((bf16[128,1024]{0,1:T(8,128)(2,1)S(1)}, bf16[128,1024]{0,1:T(8,128)(2,1)S(1)}, u32[]{:S(2)}, u32[]{:S(2)}) %collective-permute-start) | collective-permute-done | bytes 262176 | tf_op jit(solution)/shard_map/while/body/eval_jaxpr/ppermute | solution.py:15
  70.4 0.4 fusion.42
  70.9 0.3 fusion.44
  71.2 1.0 %bitcast_add_fusion.3 = f32[128,4,6,128]{3,0,2,1:T(8,128)S(1)} fusion(f32[128,4,6,128]{3,0,2,1:T(8,128)S(1)} %get-tuple-element.397, bf16[128,4,128,1]{0,2,3,1:T(8,128)(2,1)S(1)} %bitcast.62, f32[4,6,128,128]{2,3,1,0:T(8,128)S(1)} %get-tuple-element.376, f32[128,4,6]{0,2,1:T(8,128)S(1)} %get-tuple-element.378, f32[4,6,128]{2,1,0:T(8,128)S(1)} %get-tuple-element.409), kind=kOutput, calls=%fused_computation.clone.1 | convolution fusion | flops 102236160 | bytes 4874240 | tf_op jit(solution)/shard_map/while/body/eval_jaxpr/hgij,jhd->ihgd/dot_general | solution.py:40
  72.3 0.5 copy.29
  72.7 0.2 divide_convert_fusion
  72.9 2.0 %collective-permute-start.1 = (bf16[128,3072]{0,1:T(8,128)(2,1)S(1)}, bf16[128,3072]{0,1:T(8,128)(2,1)S(1)}, u32[]{:S(2)}, u32[]{:S(2)}) collective-permute-start(bf16[128,3072]{0,1:T(8,128)(2,1)S(1)} %bitcast.70), channel_id=1, source_target_pairs={{0,8},{8,16},{16,24},{24,0},{1,9},{9,17},{17,25},{25,1},{2,10},{10... | collective-permute-start | bytes 2359304 | tf_op jit(solution)/shard_map/ppermute | solution.py:15
  75.0 12.6 %collective-permute-done.1 = bf16[128,3072]{0,1:T(8,128)(2,1)S(1)} collective-permute-done((bf16[128,3072]{0,1:T(8,128)(2,1)S(1)}, bf16[128,3072]{0,1:T(8,128)(2,1)S(1)}, u32[]{:S(2)}, u32[]{:S(2)}) %collective-permute-start.1) | collective-permute-done | bytes 786464 | tf_op jit(solution)/shard_map/ppermute | solution.py:15
  87.6 1.2 %copy.30 = bf16[1,1,128,3072]{3,2,1,0:T(8,128)(2,1)} copy(bf16[1,1,128,3072]{2,3,1,0:T(8,128)(2,1)S(1)} %bitcast.69) | data formatting | bytes 1572864 | tf_op jit(solution)/shard_map/broadcast_in_dim;stack | solution.py:94
  (57 shorter events, 0.6 us)
Async XLA Ops:
  0.0 2.1 %copy-start = (bf16[1,1,128,3072]{3,2,1,0:T(8,128)(2,1)S(1)}, bf16[1,1,128,3072]{3,2,1,0:T(8,128)(2,1)}, u32[]{:S(2)}) copy-start(bf16[1,1,128,3072]{3,2,1,0:T(8,128)(2,1)} %param.5) | copy-start | bytes 2359300
  3.6 0.9 copy-start.1
  4.5 8.6 %collective-permute-start = (bf16[128,1024]{0,1:T(8,128)(2,1)S(1)}, bf16[128,1024]{0,1:T(8,128)(2,1)S(1)}, u32[]{:S(2)}, u32[]{:S(2)}) collective-permute-start(bf16[128,1024]{0,1:T(8,128)(2,1)S(1)} %get-tuple-element.394), channel_id=1, source_target_pairs={{0,1},{1,2},{2,3},{3,4},{4,5},{5,6},{6,7},{7,0},{8,9},{9,10},{10,1... | collective-permute-start | bytes 786440 | tf_op jit(solution)/shard_map/while/body/eval_jaxpr/ppermute | solution.py:15
  15.0 7.6 %collective-permute-start = (bf16[128,1024]{0,1:T(8,128)(2,1)S(1)}, bf16[128,1024]{0,1:T(8,128)(2,1)S(1)}, u32[]{:S(2)}, u32[]{:S(2)}) collective-permute-start(bf16[128,1024]{0,1:T(8,128)(2,1)S(1)} %get-tuple-element.394), channel_id=1, source_target_pairs={{0,1},{1,2},{2,3},{3,4},{4,5},{5,6},{6,7},{7,0},{8,9},{9,10},{10,1... | collective-permute-start | bytes 786440 | tf_op jit(solution)/shard_map/while/body/eval_jaxpr/ppermute | solution.py:15
  24.6 7.6 %collective-permute-start = (bf16[128,1024]{0,1:T(8,128)(2,1)S(1)}, bf16[128,1024]{0,1:T(8,128)(2,1)S(1)}, u32[]{:S(2)}, u32[]{:S(2)}) collective-permute-start(bf16[128,1024]{0,1:T(8,128)(2,1)S(1)} %get-tuple-element.394), channel_id=1, source_target_pairs={{0,1},{1,2},{2,3},{3,4},{4,5},{5,6},{6,7},{7,0},{8,9},{9,10},{10,1... | collective-permute-start | bytes 786440 | tf_op jit(solution)/shard_map/while/body/eval_jaxpr/ppermute | solution.py:15
  34.1 7.6 %collective-permute-start = (bf16[128,1024]{0,1:T(8,128)(2,1)S(1)}, bf16[128,1024]{0,1:T(8,128)(2,1)S(1)}, u32[]{:S(2)}, u32[]{:S(2)}) collective-permute-start(bf16[128,1024]{0,1:T(8,128)(2,1)S(1)} %get-tuple-element.394), channel_id=1, source_target_pairs={{0,1},{1,2},{2,3},{3,4},{4,5},{5,6},{6,7},{7,0},{8,9},{9,10},{10,1... | collective-permute-start | bytes 786440 | tf_op jit(solution)/shard_map/while/body/eval_jaxpr/ppermute | solution.py:15
  43.7 7.6 %collective-permute-start = (bf16[128,1024]{0,1:T(8,128)(2,1)S(1)}, bf16[128,1024]{0,1:T(8,128)(2,1)S(1)}, u32[]{:S(2)}, u32[]{:S(2)}) collective-permute-start(bf16[128,1024]{0,1:T(8,128)(2,1)S(1)} %get-tuple-element.394), channel_id=1, source_target_pairs={{0,1},{1,2},{2,3},{3,4},{4,5},{5,6},{6,7},{7,0},{8,9},{9,10},{10,1... | collective-permute-start | bytes 786440 | tf_op jit(solution)/shard_map/while/body/eval_jaxpr/ppermute | solution.py:15
  53.2 7.6 %collective-permute-start = (bf16[128,1024]{0,1:T(8,128)(2,1)S(1)}, bf16[128,1024]{0,1:T(8,128)(2,1)S(1)}, u32[]{:S(2)}, u32[]{:S(2)}) collective-permute-start(bf16[128,1024]{0,1:T(8,128)(2,1)S(1)} %get-tuple-element.394), channel_id=1, source_target_pairs={{0,1},{1,2},{2,3},{3,4},{4,5},{5,6},{6,7},{7,0},{8,9},{9,10},{10,1... | collective-permute-start | bytes 786440 | tf_op jit(solution)/shard_map/while/body/eval_jaxpr/ppermute | solution.py:15
  62.7 7.6 %collective-permute-start = (bf16[128,1024]{0,1:T(8,128)(2,1)S(1)}, bf16[128,1024]{0,1:T(8,128)(2,1)S(1)}, u32[]{:S(2)}, u32[]{:S(2)}) collective-permute-start(bf16[128,1024]{0,1:T(8,128)(2,1)S(1)} %get-tuple-element.394), channel_id=1, source_target_pairs={{0,1},{1,2},{2,3},{3,4},{4,5},{5,6},{6,7},{7,0},{8,9},{9,10},{10,1... | collective-permute-start | bytes 786440 | tf_op jit(solution)/shard_map/while/body/eval_jaxpr/ppermute | solution.py:15
  72.9 14.6 %collective-permute-start.1 = (bf16[128,3072]{0,1:T(8,128)(2,1)S(1)}, bf16[128,3072]{0,1:T(8,128)(2,1)S(1)}, u32[]{:S(2)}, u32[]{:S(2)}) collective-permute-start(bf16[128,3072]{0,1:T(8,128)(2,1)S(1)} %bitcast.70), channel_id=1, source_target_pairs={{0,8},{8,16},{16,24},{24,0},{1,9},{9,17},{17,25},{25,1},{2,10},{10... | collective-permute-start | bytes 2359304 | tf_op jit(solution)/shard_map/ppermute | solution.py:15
where the time goes:
time: 88.9 us; the launch traced here: 88.7 us
  waiting for transfers between devices  64.7 us (73%)
  matrix products  11.6 us (13%)
  other arithmetic  4.85 us (5%)
  local copies, waits for them, and re-layouts  3.81 us (4%)
  starting transfers between devices  2.94 us (3%)
    ppermute x8, waiting for transfers between devices, shifted(): lax.ppermute(array, axis, [(i, (i + by) % peers) for i in range(peers)])  64.7 us
    dot_general x8, matrix products, tile_update(): jnp.einsum('hgij,jhd->ihgd', weights, value_rows, preferred_element_type=...  8.07 us
    dot_general x8, matrix products, tile_update(): jnp.einsum('ihgd,jhd->hgij', query_rows, key_rows, preferred_element_type...  3.54 us
    ppermute x8, starting transfers between devices, shifted(): lax.ppermute(array, axis, [(i, (i + by) % peers) for i in range(peers)])  2.94 us
    reduce_sum x8, other arithmetic, tile_update(): new_total = run_total * factor + jnp.sum(expo, axis=3)  2.27 us
  transfers between devices with their start and end apart: 8, of which 8 were waited for; matrix products, arithmetic and copies ran while one was open for 1% of the time, Pallas kernels for 0%

commit v1 on v0

v1 whole, which is shorter than its diff:
```python
import functools
import math

import jax
import jax.numpy as jnp
from jax import lax
from jax.experimental import pallas as pl
from jax.experimental.pallas import tpu as pltpu
from jax.sharding import PartitionSpec as P

HEAD_SIZE = 128
MESH = pl.DeviceIdType.MESH
STACK = 2
LEAD = 2


def kernel(
    n, sections, key_heads, per_kv,
    layout_ref, q_hbm, kv_hbm, out_ref,
    q_buf, kv_all, att, bias, local_sem, send_sem, recv_sem, out_send, out_recv,
):
    rows = q_buf.shape[0]
    block = rows // 2
    chips = n // 2
    section = lax.axis_index("pipe")
    me = lax.axis_index("ctx")
    place = me // 2
    core = me % 2
    width = key_heads * HEAD_SIZE

    def at_ctx(index):
        return {"pipe": section, "ctx": index}

    after = (section + 1) % sections
    before = (section + sections - 1) % sections
    has_right = place < chips - 1
    has_left = place > 0
    sibling = 2 * place + 1 - core

    def own_copy(head, half):
        return pltpu.make_async_copy(
            kv_hbm.at[:, pl.ds(half * width + head * HEAD_SIZE, HEAD_SIZE)],
            kv_all.at[head, me, :, pl.ds(half * HEAD_SIZE, HEAD_SIZE)],
            local_sem.at[2 * head + half],
        )

    q_copy = pltpu.make_async_copy(q_hbm, q_buf, local_sem.at[2 * key_heads])
    for head in range(key_heads):
        own_copy(head, 0).start()
        own_copy(head, 1).start()
    q_copy.start()

    barrier = pltpu.get_barrier_semaphore()
    pl.semaphore_signal(barrier, inc=1, device_id=at_ctx(sibling), device_id_type=MESH)
    for other in (after, before):
        pl.semaphore_signal(
            barrier, inc=1, device_id={"pipe": other, "ctx": me}, device_id_type=MESH
        )

    @pl.when(has_right)
    def _():
        pl.semaphore_signal(barrier, inc=1, device_id=at_ctx(me + 2), device_id_type=MESH)

    @pl.when(has_left)
    def _():
        pl.semaphore_signal(barrier, inc=1, device_id=at_ctx(me - 2), device_id_type=MESH)

    for head in range(key_heads):
        own_copy(head, 0).wait()
        own_copy(head, 1).wait()
    pl.semaphore_wait(
        barrier, 3 + has_right.astype(jnp.int32) + has_left.astype(jnp.int32)
    )

    def piece(head, origin, way):
        target = (me + 2, me - 2, sibling)[way]
        return pltpu.make_async_remote_copy(
            src_ref=kv_all.at[head, origin],
            dst_ref=kv_all.at[head, origin],
            send_sem=send_sem.at[way, head, origin],
            recv_sem=recv_sem.at[head, origin],
            device_id=at_ctx(target),
            device_id_type=MESH,
        )

    def send_own(head):
        @pl.when(has_right)
        def _():
            piece(head, me, 0).start()

        @pl.when(has_left)
        def _():
            piece(head, me, 1).start()

        piece(head, me, 2).start()

    def hop(head, step):
        @pl.when(place >= step)
        def _():
            origin = me - 2 * step
            piece(head, origin, 2).wait_recv()

            @pl.when(has_right)
            def _():
                piece(head, origin, 0).start()

            piece(head, origin, 2).start()

        @pl.when(place + step < chips)
        def _():
            origin = me + 2 * step
            piece(head, origin, 2).wait_recv()

            @pl.when(has_left)
            def _():
                piece(head, origin, 1).start()

            piece(head, origin, 2).start()

    def hops(head, low, high):
        lax.fori_loop(low, high, lambda step, c: (hop(head, step), c)[1], 0)

    for head in range(min(LEAD, key_heads)):
        send_own(head)

    row_in = lax.broadcasted_iota(jnp.int32, (rows, rows), 0)
    col_in = lax.broadcasted_iota(jnp.int32, (rows, rows), 1)

    def positions(owner, iota):
        first = layout_ref[0, 0, 2 * owner]
        second = layout_ref[0, 0, 2 * owner + 1]
        return jnp.where(iota < block, first * block + iota, (second - 1) * block + iota)

    query_pos = positions(me, row_in)
    for owner in range(n):
        key_pos = positions(owner, col_in)
        bias[:, owner * rows:(owner + 1) * rows] = jnp.where(key_pos <= query_pos, 0.0, -1e30)

    q_copy.wait()
    hops(0, 1, chips)

    def out_copy(index):
        columns = pl.ds(pl.multiple_of(index * HEAD_SIZE, HEAD_SIZE), HEAD_SIZE)
        return pltpu.make_async_remote_copy(
            src_ref=att.at[:, columns],
            dst_ref=out_ref.at[:, columns],
            send_sem=out_send.at[index],
            recv_sem=out_recv.at[index],
            device_id={"pipe": after, "ctx": me},
            device_id_type=MESH,
        )

    scale = 1.0 / math.sqrt(HEAD_SIZE)
    groups = per_kv // STACK

    for head in range(key_heads):
        if head + LEAD < key_heads:
            send_own(head + LEAD)

        def sibling_wait(chip, c, head=head):
            piece(head, 2 * chip + 1 - core, 2).wait_recv()
            return c

        lax.fori_loop(0, chips, sibling_wait, 0)

        def group(g, c, head=head):
            first = head * per_kv + g * STACK
            keys = kv_all[head, :, :, :HEAD_SIZE].reshape(n * rows, HEAD_SIZE)
            values = kv_all[head, :, :, HEAD_SIZE:].reshape(n * rows, HEAD_SIZE)
            base = pl.multiple_of(first * HEAD_SIZE, HEAD_SIZE)
            q_rows = jnp.concatenate(
                [q_buf[:, pl.ds(base + i * HEAD_SIZE, HEAD_SIZE)] for i in range(STACK)], axis=0
            )
            scores = lax.dot_general(
                q_rows, keys, (((1,), (1,)), ((), ())), preferred_element_type=jnp.float32
            )
            scores = scores.reshape(STACK, rows, n * rows) * scale + bias[...][None]
            row_max = jnp.max(scores, axis=2, keepdims=True)
            expo = jnp.exp(scores - row_max)
            total = jnp.sum(expo, axis=2, keepdims=True)
            weights = expo.astype(jnp.bfloat16).reshape(STACK * rows, n * rows)
            product = jnp.dot(weights, values, preferred_element_type=jnp.float32)
            result = (product.reshape(STACK, rows, HEAD_SIZE) / total).astype(jnp.bfloat16)
            for i in range(STACK):
                att[:, pl.ds(base + i * HEAD_SIZE, HEAD_SIZE)] = result[i]
            for i in range(STACK):
                out_copy(first + i).start()
            if head + 1 < key_heads:
                hops(
                    head + 1,
                    1 + g * (chips - 1) // groups,
                    1 + (g + 1) * (chips - 1) // groups,
                )
            return c

        lax.fori_loop(0, groups, group, 0)

    def finish_piece(head, origin, right, left):
        @pl.when(jnp.logical_and(right, has_right))
        def _():
            piece(head, origin, 0).wait_send()

        @pl.when(jnp.logical_and(left, has_left))
        def _():
            piece(head, origin, 1).wait_send()

        piece(head, origin, 2).wait_send()

    for head in range(key_heads):
        def finish(chip, c, head=head):
            finish_piece(head, 2 * chip + core, chip <= place, chip >= place)
            return c

        lax.fori_loop(0, chips, finish, 0)

    def finish_out(index, c):
        out_copy(index).wait()
        return c

    lax.fori_loop(0, key_heads * per_kv, finish_out, 0)


def on_device(queries, projected_key_value, layout):
    rows, width = queries.shape[2:]
    kv_width = projected_key_value.shape[3]
    key_heads = kv_width // (2 * HEAD_SIZE)
    per_kv = width // (key_heads * HEAD_SIZE)
    heads = key_heads * per_kv
    n = lax.axis_size("ctx")
    sections = lax.axis_size("pipe")
    out = pl.pallas_call(
        functools.partial(kernel, n, sections, key_heads, per_kv),
        out_shape=jax.ShapeDtypeStruct((rows, width), jnp.bfloat16),
        in_specs=[
            pl.BlockSpec(memory_space=pltpu.SMEM),
            pl.BlockSpec(memory_space=pl.ANY),
            pl.BlockSpec(memory_space=pl.ANY),
        ],
        out_specs=pl.BlockSpec(memory_space=pl.ANY),
        scratch_shapes=[
            pltpu.VMEM((rows, width), jnp.bfloat16),
            pltpu.VMEM((key_heads, n, rows, 2 * HEAD_SIZE), jnp.bfloat16),
            pltpu.VMEM((rows, width), jnp.bfloat16),
            pltpu.VMEM((rows, n * rows), jnp.float32),
            pltpu.SemaphoreType.DMA((2 * key_heads + 1,)),
            pltpu.SemaphoreType.DMA((3, key_heads, n)),
            pltpu.SemaphoreType.DMA((key_heads, n)),
            pltpu.SemaphoreType.DMA((heads,)),
            pltpu.SemaphoreType.DMA((heads,)),
        ],
        compiler_params=pltpu.CompilerParams(
            collective_id=0, has_side_effects=True, vmem_limit_bytes=60 * 1024 * 1024
        ),
        name="gather_attend_relay",
    )(layout, queries.reshape(rows, width), projected_key_value.reshape(rows, kv_width))
    return out.reshape(queries.shape)


def solution(mesh):
    placed = (P("pipe", None, "ctx", None), P("pipe", None, "ctx", None), P())
    return jax.shard_map(
        on_device,
        mesh=mesh,
        in_specs=placed,
        out_specs=P("pipe", None, "ctx", None),
        check_vma=False,
    )
```

time: 88.9 us -> 43.2 us (0.49)
  waiting for transfers between devices: 64.7 us -> 0 us
  Pallas kernels: 0 us -> 40.9 us
  matrix products: 11.6 us -> 0 us
  other arithmetic: 4.85 us -> 0 us
  starting transfers between devices: 2.94 us -> 0 us
  local copies, waits for them, and re-layouts: 3.81 us -> 2.06 us
    ppermute x8 -> x0, waiting for transfers between devices: 64.7 us -> none  [shifted(): lax.ppermute(array, axis, [(i, (i + by) % peers) for i in range(peers)])]
    pallas_call x0 -> x1, Pallas kernels: none -> 40.9 us  [on_device(): pl.pallas_call(functools.partial(kernel, n, sections, key_heads, per_kv),...]
    dot_general x16 -> x0, matrix products: 11.6 us -> none  [the longest x8 8.07 us: tile_update(): jnp.einsum('hgij,jhd->ihgd', weights, value_rows, preferred_element_type=...]
    reduce_sum x16 -> x0, other arithmetic: 3.69 us -> none  [the longest x8 2.27 us: tile_update(): new_total = run_total * factor + jnp.sum(expo, axis=3)]
    ppermute x8 -> x0, starting transfers between devices: 2.94 us -> none  [shifted(): lax.ppermute(array, axis, [(i, (i + by) % peers) for i in range(peers)])]
    another operation x1 -> x0, local copies, waits for them, and re-layouts: 1.16 us -> none  [on_device(): return jnp.stack(results)[None]]
    while x16 -> x0, local copies, waits for them, and re-layouts: 1.01 us -> none  [the longest x2 0.85 us: on_device(): carry = lax.fori_loop(1, seq_devs, cycle_hop, (own_piece, carry))[1]]
    unnamed x6 -> x1, local copies, waits for them, and re-layouts: 1.5 us -> 2.06 us
  transfers between devices with their start and end apart: 8 -> 0, of which waited for: 8 -> 0; matrix products, arithmetic and copies ran while one was open for 1% -> 0% of each run, Pallas kernels for 0% -> 0%
where the time goes in v1:
time: 43.2 us; the launch traced here: 43 us
  Pallas kernels  40.9 us (95%)
  local copies, waits for them, and re-layouts  2.06 us (5%)
    pallas_call x1, Pallas kernels, on_device(): pl.pallas_call(functools.partial(kernel, n, sections, key_heads, per_kv),...  40.9 us
    unnamed x1, local copies, waits for them, and re-layouts  2.06 us

profile of v1, /device:TPU:0, one launch (start us, length us, event | category | flops | bytes accessed | tf_op | source)
XLA Modules:
  0.0 43.0 jit_solution(13246770182912160362)
XLA Ops:
  0.0 40.9 %gather_attend_relay.1 = bf16[128,3072]{1,0:T(8,128)(2,1)} custom-call(s32[1,1,16]{2,1,0:T(1,128)} %layout_ref.1, bf16[128,3072]{1,0:T(8,128)(2,1)} %bitcast.4, bf16[128,1024]{1,0:T(8,128)(2,1)} %bitcast.5), custom_call_target="tpu_custom_call" | custom-call | tf_op jit(solution)/shard_map/gather_attend_relay/pallas_call | solution.py:231
  41.0 2.1 %copy.5 = bf16[1,1,128,3072]{3,2,1,0:T(8,128)(2,1)} copy(bf16[1,1,128,3072]{3,2,1,0:T(8,128)(2,1)} %bitcast.3) | data formatting | bytes 1572864

commit v2 on v1

--- a/solution.py
+++ b/solution.py
@@ -12,12 +12,13 @@
 MESH = pl.DeviceIdType.MESH
 STACK = 2
 LEAD = 2
+SHIP = 2
 
 
 def kernel(
     n, sections, key_heads, per_kv,
     layout_ref, q_hbm, kv_hbm, out_ref,
-    q_buf, kv_all, att, bias, local_sem, send_sem, recv_sem, out_send, out_recv,
+    q_buf, kv_all, att, bias, local_sem, send_sem, recv_sem, out_send, out_recv, ship_send, ship_recv,
 ):
     rows = q_buf.shape[0]
     block = rows // 2
@@ -27,6 +28,8 @@
     place = me // 2
     core = me % 2
     width = key_heads * HEAD_SIZE
+    stay = key_heads - min(SHIP, key_heads - 1)
+    head_width = per_kv * HEAD_SIZE
 
     def at_ctx(index):
         return {"pipe": section, "ctx": index}
@@ -44,8 +47,27 @@
             local_sem.at[2 * head + half],
         )
 
-    q_copy = pltpu.make_async_copy(q_hbm, q_buf, local_sem.at[2 * key_heads])
-    for head in range(key_heads):
+    def ship_copy(head, what):
+        if what == 2:
+            columns = pl.ds(head * head_width, head_width)
+            source, target = q_hbm.at[:, columns], q_buf.at[:, columns]
+        else:
+            source = kv_hbm.at[:, pl.ds(what * width + head * HEAD_SIZE, HEAD_SIZE)]
+            target = kv_all.at[head, me, :, pl.ds(what * HEAD_SIZE, HEAD_SIZE)]
+        return pltpu.make_async_remote_copy(
+            src_ref=source,
+            dst_ref=target,
+            send_sem=ship_send.at[head, what],
+            recv_sem=ship_recv.at[head, what],
+            device_id={"pipe": after, "ctx": me},
+            device_id_type=MESH,
+        )
+
+    q_columns = pl.ds(0, stay * head_width)
+    q_copy = pltpu.make_async_copy(
+        q_hbm.at[:, q_columns], q_buf.at[:, q_columns], local_sem.at[2 * key_heads]
+    )
+    for head in range(stay):
         own_copy(head, 0).start()
         own_copy(head, 1).start()
     q_copy.start()
@@ -65,12 +87,15 @@
     def _():
         pl.semaphore_signal(barrier, inc=1, device_id=at_ctx(me - 2), device_id_type=MESH)
 
-    for head in range(key_heads):
+    for head in range(stay):
         own_copy(head, 0).wait()
         own_copy(head, 1).wait()
     pl.semaphore_wait(
         barrier, 3 + has_right.astype(jnp.int32) + has_left.astype(jnp.int32)
     )
+    for head in range(stay, key_heads):
+        ship_copy(head, 0).start()
+        ship_copy(head, 1).start()
 
     def piece(head, origin, way):
         target = (me + 2, me - 2, sibling)[way]
@@ -84,6 +109,10 @@
         )
 
     def send_own(head):
+        if head >= stay:
+            ship_copy(head, 0).wait_recv()
+            ship_copy(head, 1).wait_recv()
+
         @pl.when(has_right)
         def _():
             piece(head, me, 0).start()
@@ -117,11 +146,22 @@
 
             piece(head, origin, 2).start()
 
-    def hops(head, low, high):
-        lax.fori_loop(low, high, lambda step, c: (hop(head, step), c)[1], 0)
-
-    for head in range(min(LEAD, key_heads)):
-        send_own(head)
+    def steps_of(wave):
+        return max(1, wave - key_heads + 1), min(wave, chips - 1) + 1
+
+    def hops(wave, low, high):
+        lax.fori_loop(low, high, lambda step, c: (hop(wave - step, step), c)[1], 0)
+
+    def own_of(wave):
+        if wave == 0:
+            for head in range(min(LEAD, key_heads)):
+                send_own(head)
+        elif wave + LEAD - 1 < key_heads:
+            send_own(wave + LEAD - 1)
+
+    own_of(0)
+    for head in range(stay, key_heads):
+        ship_copy(head, 2).start()
 
     row_in = lax.broadcasted_iota(jnp.int32, (rows, rows), 0)
     col_in = lax.broadcasted_iota(jnp.int32, (rows, rows), 1)
@@ -137,7 +177,9 @@
         bias[:, owner * rows:(owner + 1) * rows] = jnp.where(key_pos <= query_pos, 0.0, -1e30)
 
     q_copy.wait()
-    hops(0, 1, chips)
+    for wave in range(1, chips):
+        own_of(wave)
+        hops(wave, *steps_of(wave))
 
     def out_copy(index):
         columns = pl.ds(pl.multiple_of(index * HEAD_SIZE, HEAD_SIZE), HEAD_SIZE)
@@ -153,9 +195,18 @@
     scale = 1.0 / math.sqrt(HEAD_SIZE)
     groups = per_kv // STACK
 
+    def home_copy(index):
+        columns = pl.ds(pl.multiple_of(index * HEAD_SIZE, HEAD_SIZE), HEAD_SIZE)
+        return pltpu.make_async_copy(
+            att.at[:, columns], out_ref.at[:, columns], out_send.at[index]
+        )
+
     for head in range(key_heads):
-        if head + LEAD < key_heads:
-            send_own(head + LEAD)
+        wave = head + chips
+        own_of(wave)
+        low, high = steps_of(wave)
+        if head >= stay:
+            ship_copy(head, 2).wait_recv()
 
         def sibling_wait(chip, c, head=head):
             piece(head, 2 * chip + 1 - core, 2).wait_recv()
@@ -163,7 +214,7 @@
 
         lax.fori_loop(0, chips, sibling_wait, 0)
 
-        def group(g, c, head=head):
+        def group(g, c, head=head, wave=wave, low=low, high=high):
             first = head * per_kv + g * STACK
             keys = kv_all[head, :, :, :HEAD_SIZE].reshape(n * rows, HEAD_SIZE)
             values = kv_all[head, :, :, HEAD_SIZE:].reshape(n * rows, HEAD_SIZE)
@@ -184,12 +235,12 @@
             for i in range(STACK):
                 att[:, pl.ds(base + i * HEAD_SIZE, HEAD_SIZE)] = result[i]
             for i in range(STACK):
-                out_copy(first + i).start()
-            if head + 1 < key_heads:
+                (out_copy if head < stay else home_copy)(first + i).start()
+            if high > low:
                 hops(
-                    head + 1,
-                    1 + g * (chips - 1) // groups,
-                    1 + (g + 1) * (chips - 1) // groups,
+                    wave,
+                    low + g * (high - low) // groups,
+                    low + (g + 1) * (high - low) // groups,
                 )
             return c
 
@@ -217,7 +268,15 @@
         out_copy(index).wait()
         return c
 
-    lax.fori_loop(0, key_heads * per_kv, finish_out, 0)
+    def finish_home(index, c):
+        home_copy(index).wait()
+        return c
+
+    lax.fori_loop(stay * per_kv, key_heads * per_kv, finish_home, 0)
+    for head in range(stay, key_heads):
+        for what in range(3):
+            ship_copy(head, what).wait_send()
+    lax.fori_loop(0, stay * per_kv, finish_out, 0)
 
 
 def on_device(queries, projected_key_value, layout):
@@ -247,6 +306,8 @@
             pltpu.SemaphoreType.DMA((key_heads, n)),
             pltpu.SemaphoreType.DMA((heads,)),
             pltpu.SemaphoreType.DMA((heads,)),
+            pltpu.SemaphoreType.DMA((key_heads, 3)),
+            pltpu.SemaphoreType.DMA((key_heads, 3)),
         ],
         compiler_params=pltpu.CompilerParams(
             collective_id=0, has_side_effects=True, vmem_limit_bytes=60 * 1024 * 1024

time: 43.2 us -> 35.7 us (0.83)
  Pallas kernels: 40.9 us -> 33.5 us
    pallas_call x1, Pallas kernels: 40.9 us -> 33.5 us  [on_device(): pl.pallas_call(functools.partial(kernel, n, sections, key_heads, per_kv),...]
where the time goes in v2:
time: 35.7 us; the launch traced here: 35.6 us
  Pallas kernels  33.5 us (94%)
  local copies, waits for them, and re-layouts  2.06 us (6%)
    pallas_call x1, Pallas kernels, on_device(): pl.pallas_call(functools.partial(kernel, n, sections, key_heads, per_kv),...  33.5 us
    unnamed x1, local copies, waits for them, and re-layouts  2.06 us

profile of v2, /device:TPU:0, one launch (start us, length us, event | category | flops | bytes accessed | tf_op | source)
XLA Modules:
  0.0 35.6 jit_solution(8755849902370741137)
XLA Ops:
  0.0 33.5 %gather_attend_relay.1 = bf16[128,3072]{1,0:T(8,128)(2,1)} custom-call(s32[1,1,16]{2,1,0:T(1,128)} %layout_ref.1, bf16[128,3072]{1,0:T(8,128)(2,1)} %bitcast.4, bf16[128,1024]{1,0:T(8,128)(2,1)} %bitcast.5), custom_call_target="tpu_custom_call" | custom-call | tf_op jit(solution)/shard_map/gather_attend_relay/pallas_call | solution.py:290
  33.5 2.1 %copy.5 = bf16[1,1,128,3072]{3,2,1,0:T(8,128)(2,1)} copy(bf16[1,1,128,3072]{3,2,1,0:T(8,128)(2,1)} %bitcast.3) | data formatting | bytes 1572864

commit v3 on v2

--- a/solution.py
+++ b/solution.py
@@ -13,6 +13,8 @@
 STACK = 2
 LEAD = 2
 SHIP = 2
+SHIP_LEAD = 2
+LAST_STACK = 6
 
 
 def kernel(
@@ -154,10 +156,14 @@
 
     def own_of(wave):
         if wave == 0:
-            for head in range(min(LEAD, key_heads)):
+            for head in range(min(LEAD, stay)):
                 send_own(head)
-        elif wave + LEAD - 1 < key_heads:
+            return
+        if LEAD <= wave + LEAD - 1 < stay:
             send_own(wave + LEAD - 1)
+        for head in range(stay, key_heads):
+            if max(head + 1 - SHIP_LEAD, 1) == wave:
+                send_own(head)
 
     own_of(0)
     for head in range(stay, key_heads):
@@ -178,8 +184,8 @@
 
     q_copy.wait()
     for wave in range(1, chips):
+        hops(wave, *steps_of(wave))
         own_of(wave)
-        hops(wave, *steps_of(wave))
 
     def out_copy(index):
         columns = pl.ds(pl.multiple_of(index * HEAD_SIZE, HEAD_SIZE), HEAD_SIZE)
@@ -193,7 +199,6 @@
         )
 
     scale = 1.0 / math.sqrt(HEAD_SIZE)
-    groups = per_kv // STACK
 
     def home_copy(index):
         columns = pl.ds(pl.multiple_of(index * HEAD_SIZE, HEAD_SIZE), HEAD_SIZE)
@@ -203,6 +208,8 @@
 
     for head in range(key_heads):
         wave = head + chips
+        stack = LAST_STACK if head == key_heads - 1 else STACK
+        groups = per_kv // stack
         own_of(wave)
         low, high = steps_of(wave)
         if head >= stay:
@@ -214,27 +221,27 @@
 
         lax.fori_loop(0, chips, sibling_wait, 0)
 
-        def group(g, c, head=head, wave=wave, low=low, high=high):
-            first = head * per_kv + g * STACK
+        def group(g, c, head=head, wave=wave, low=low, high=high, stack=stack, groups=groups):
+            first = head * per_kv + g * stack
             keys = kv_all[head, :, :, :HEAD_SIZE].reshape(n * rows, HEAD_SIZE)
             values = kv_all[head, :, :, HEAD_SIZE:].reshape(n * rows, HEAD_SIZE)
             base = pl.multiple_of(first * HEAD_SIZE, HEAD_SIZE)
             q_rows = jnp.concatenate(
-                [q_buf[:, pl.ds(base + i * HEAD_SIZE, HEAD_SIZE)] for i in range(STACK)], axis=0
+                [q_buf[:, pl.ds(base + i * HEAD_SIZE, HEAD_SIZE)] for i in range(stack)], axis=0
             )
             scores = lax.dot_general(
                 q_rows, keys, (((1,), (1,)), ((), ())), preferred_element_type=jnp.float32
             )
-            scores = scores.reshape(STACK, rows, n * rows) * scale + bias[...][None]
+            scores = scores.reshape(stack, rows, n * rows) * scale + bias[...][None]
             row_max = jnp.max(scores, axis=2, keepdims=True)
             expo = jnp.exp(scores - row_max)
             total = jnp.sum(expo, axis=2, keepdims=True)
-            weights = expo.astype(jnp.bfloat16).reshape(STACK * rows, n * rows)
+            weights = expo.astype(jnp.bfloat16).reshape(stack * rows, n * rows)
             product = jnp.dot(weights, values, preferred_element_type=jnp.float32)
-            result = (product.reshape(STACK, rows, HEAD_SIZE) / total).astype(jnp.bfloat16)
-            for i in range(STACK):
+            result = (product.reshape(stack, rows, HEAD_SIZE) / total).astype(jnp.bfloat16)
+            for i in range(stack):
                 att[:, pl.ds(base + i * HEAD_SIZE, HEAD_SIZE)] = result[i]
-            for i in range(STACK):
+            for i in range(stack):
                 (out_copy if head < stay else home_copy)(first + i).start()
             if high > low:
                 hops(
@@ -279,6 +286,27 @@
     lax.fori_loop(0, stay * per_kv, finish_out, 0)
 
 
+def write(parts, source, target, sem):
+    share = source.shape[0] // parts
+    copies = [
+        pltpu.make_async_copy(
+            source.at[pl.ds(i * share, share)], target.at[pl.ds(i * share, share)], sem.at[i]
+        )
+        for i in range(parts)
+    ]
+    for copy in copies:
+        copy.start()
+    for copy in copies:
+        copy.wait()
+
+
+def vmem_bytes(n, rows, width, kv_width):
+    keys = n * rows
+    gathered = 2 * keys * kv_width
+    scores = 4 * rows * keys
+    return gathered + 3 * 2 * rows * width + (3 * max(STACK, LAST_STACK) + 2) * scores + 2 * 1024 * 1024
+
+
 def on_device(queries, projected_key_value, layout):
     rows, width = queries.shape[2:]
     kv_width = projected_key_value.shape[3]
@@ -287,15 +315,15 @@
     heads = key_heads * per_kv
     n = lax.axis_size("ctx")
     sections = lax.axis_size("pipe")
-    out = pl.pallas_call(
+    arrived = pl.pallas_call(
         functools.partial(kernel, n, sections, key_heads, per_kv),
         out_shape=jax.ShapeDtypeStruct((rows, width), jnp.bfloat16),
         in_specs=[
             pl.BlockSpec(memory_space=pltpu.SMEM),
-            pl.BlockSpec(memory_space=pl.ANY),
-            pl.BlockSpec(memory_space=pl.ANY),
+            pl.BlockSpec(memory_space=pltpu.HBM),
+            pl.BlockSpec(memory_space=pltpu.HBM),
         ],
-        out_specs=pl.BlockSpec(memory_space=pl.ANY),
+        out_specs=pl.BlockSpec(memory_space=pltpu.VMEM),
         scratch_shapes=[
             pltpu.VMEM((rows, width), jnp.bfloat16),
             pltpu.VMEM((key_heads, n, rows, 2 * HEAD_SIZE), jnp.bfloat16),
@@ -310,10 +338,26 @@
             pltpu.SemaphoreType.DMA((key_heads, 3)),
         ],
         compiler_params=pltpu.CompilerParams(
-            collective_id=0, has_side_effects=True, vmem_limit_bytes=60 * 1024 * 1024
+            collective_id=0, has_side_effects=True, vmem_limit_bytes=vmem_bytes(n, rows, width, kv_width)
         ),
         name="gather_attend_relay",
-    )(layout, queries.reshape(rows, width), projected_key_value.reshape(rows, kv_width))
+    )(
+        pltpu.with_memory_space_constraint(layout, pltpu.HBM),
+        pltpu.with_memory_space_constraint(queries.reshape(rows, width), pltpu.HBM),
+        pltpu.with_memory_space_constraint(
+            projected_key_value.reshape(rows, kv_width), pltpu.HBM
+        ),
+    )
+    parts = 8
+    out = pl.pallas_call(
+        functools.partial(write, parts),
+        out_shape=jax.ShapeDtypeStruct((rows, width), jnp.bfloat16),
+        in_specs=[pl.BlockSpec(memory_space=pltpu.VMEM)],
+        out_specs=pl.BlockSpec(memory_space=pltpu.HBM),
+        scratch_shapes=[pltpu.SemaphoreType.DMA((parts,))],
+        compiler_params=pltpu.CompilerParams(vmem_limit_bytes=8 * 1024 * 1024),
+        name="write_back",
+    )(arrived)
     return out.reshape(queries.shape)
 
 

time: 35.7 us -> 34.2 us (0.958)
  the two profiles are of different devices: /device:TPU:0 before, /device:TPU:1 now
where the time goes in v3:
time: 34.2 us; the launch traced here: 34.1 us
  Pallas kernels  34.1 us (100%)
    pallas_call x1, Pallas kernels, on_device(): pl.pallas_call(functools.partial(kernel, n, sections, key_heads, per_kv),...  33.1 us
    pallas_call x1, Pallas kernels, on_device(): pl.pallas_call(functools.partial(write, parts), out_shape=jax.ShapeDtypeS...  0.94 us

profile of v3, /device:TPU:1, one launch (start us, length us, event | category | flops | bytes accessed | tf_op | source)
XLA Modules:
  0.0 34.1 jit_solution(13753213872810870033)
XLA Ops:
  0.0 33.1 %gather_attend_relay.1.source = bf16[128,3072]{1,0:T(8,128)(2,1)S(1)} custom-call(s32[1,1,16]{2,1,0:T(1,128)} %layout_ref.1, bf16[128,3072]{1,0:T(8,128)(2,1)} %bitcast.3, bf16[128,1024]{1,0:T(8,128)(2,1)} %bitcast.4), custom_call_target="tpu_custom_call" | custom-call | tf_op jit(solution)/shard_map/gather_attend_relay/pallas_call | solution.py:318
  33.1 0.9 %write_back.1 = bf16[128,3072]{1,0:T(8,128)(2,1)} custom-call(bf16[128,3072]{1,0:T(8,128)(2,1)S(1)} %gather_attend_relay.1.source), custom_call_target="tpu_custom_call" | custom-call | tf_op jit(solution)/shard_map/write_back/pallas_call | solution.py:352

commit v4 on v3

--- a/solution.py
+++ b/solution.py
@@ -41,6 +41,8 @@
     has_right = place < chips - 1
     has_left = place > 0
     sibling = 2 * place + 1 - core
+    far_right = place < chips - 2
+    far_left = place > 1
 
     def own_copy(head, half):
         return pltpu.make_async_copy(
@@ -89,18 +91,28 @@
     def _():
         pl.semaphore_signal(barrier, inc=1, device_id=at_ctx(me - 2), device_id_type=MESH)
 
+    @pl.when(far_right)
+    def _():
+        pl.semaphore_signal(barrier, inc=1, device_id=at_ctx(me + 4), device_id_type=MESH)
+
+    @pl.when(far_left)
+    def _():
+        pl.semaphore_signal(barrier, inc=1, device_id=at_ctx(me - 4), device_id_type=MESH)
+
     for head in range(stay):
         own_copy(head, 0).wait()
         own_copy(head, 1).wait()
     pl.semaphore_wait(
-        barrier, 3 + has_right.astype(jnp.int32) + has_left.astype(jnp.int32)
+        barrier,
+        3 + has_right.astype(jnp.int32) + has_left.astype(jnp.int32)
+        + far_right.astype(jnp.int32) + far_left.astype(jnp.int32),
     )
     for head in range(stay, key_heads):
         ship_copy(head, 0).start()
         ship_copy(head, 1).start()
 
     def piece(head, origin, way):
-        target = (me + 2, me - 2, sibling)[way]
+        target = (me + 2, me - 2, sibling, me + 4, me - 4)[way]
         return pltpu.make_async_remote_copy(
             src_ref=kv_all.at[head, origin],
             dst_ref=kv_all.at[head, origin],
@@ -123,6 +135,14 @@
         def _():
             piece(head, me, 1).start()
 
+        @pl.when(far_right)
+        def _():
+            piece(head, me, 3).start()
+
+        @pl.when(far_left)
+        def _():
+            piece(head, me, 4).start()
+
         piece(head, me, 2).start()
 
     def hop(head, step):
@@ -131,7 +151,7 @@
             origin = me - 2 * step
             piece(head, origin, 2).wait_recv()
 
-            @pl.when(has_right)
+            @pl.when(jnp.logical_and(has_right, step > 1))
             def _():
                 piece(head, origin, 0).start()
 
@@ -142,7 +162,7 @@
             origin = me + 2 * step
             piece(head, origin, 2).wait_recv()
 
-            @pl.when(has_left)
+            @pl.when(jnp.logical_and(has_left, step > 1))
             def _():
                 piece(head, origin, 1).start()
 
@@ -266,10 +286,22 @@
 
     for head in range(key_heads):
         def finish(chip, c, head=head):
-            finish_piece(head, 2 * chip + core, chip <= place, chip >= place)
+            finish_piece(
+                head, 2 * chip + core,
+                jnp.logical_and(chip <= place, chip != place - 1),
+                jnp.logical_and(chip >= place, chip != place + 1),
+            )
             return c
 
         lax.fori_loop(0, chips, finish, 0)
+
+        @pl.when(far_right)
+        def _(head=head):
+            piece(head, me, 3).wait_send()
+
+        @pl.when(far_left)
+        def _(head=head):
+            piece(head, me, 4).wait_send()
 
     def finish_out(index, c):
         out_copy(index).wait()
@@ -330,7 +362,7 @@
             pltpu.VMEM((rows, width), jnp.bfloat16),
             pltpu.VMEM((rows, n * rows), jnp.float32),
             pltpu.SemaphoreType.DMA((2 * key_heads + 1,)),
-            pltpu.SemaphoreType.DMA((3, key_heads, n)),
+            pltpu.SemaphoreType.DMA((5, key_heads, n)),
             pltpu.SemaphoreType.DMA((key_heads, n)),
             pltpu.SemaphoreType.DMA((heads,)),
             pltpu.SemaphoreType.DMA((heads,)),

time: 34.2 us -> 38.4 us (1.12)
  Pallas kernels: 34.1 us -> 38.3 us
    pallas_call x1, Pallas kernels: 33.1 us -> 37.3 us  [on_device(): pl.pallas_call(functools.partial(kernel, n, sections, key_heads, per_kv),...]
where the time goes in v4:
time: 38.4 us; the launch traced here: 38.3 us
  Pallas kernels  38.3 us (100%)
    pallas_call x1, Pallas kernels, on_device(): pl.pallas_call(functools.partial(kernel, n, sections, key_heads, per_kv),...  37.3 us
    pallas_call x1, Pallas kernels, on_device(): pl.pallas_call(functools.partial(write, parts), out_shape=jax.ShapeDtypeS...  0.94 us

profile of v4, /device:TPU:1, one launch (start us, length us, event | category | flops | bytes accessed | tf_op | source)
XLA Modules:
  0.0 38.3 jit_solution(3834962631298767825)
XLA Ops:
  0.0 37.3 %gather_attend_relay.1.source = bf16[128,3072]{1,0:T(8,128)(2,1)S(1)} custom-call(s32[1,1,16]{2,1,0:T(1,128)} %layout_ref.1, bf16[128,3072]{1,0:T(8,128)(2,1)} %bitcast.3, bf16[128,1024]{1,0:T(8,128)(2,1)} %bitcast.4), custom_call_target="tpu_custom_call" | custom-call | tf_op jit(solution)/shard_map/gather_attend_relay/pallas_call | solution.py:350
  37.4 0.9 %write_back.1 = bf16[128,3072]{1,0:T(8,128)(2,1)} custom-call(bf16[128,3072]{1,0:T(8,128)(2,1)S(1)} %gather_attend_relay.1.source), custom_call_target="tpu_custom_call" | custom-call | tf_op jit(solution)/shard_map/write_back/pallas_call | solution.py:384
